TPU v7x, 32 devices: a whole 2x2x4 slice. The times are simulated.
32 devices in a mesh: occ: 4 (over z), vir: 8 (over y, x, core).
Axes of the slice: x: 2, y: 2, z: 4, core: 2. Of those that a mesh axis runs over, the one named last changes fastest.
Arguments:
- amplitudes: bfloat16 [40, 40, 400, 400], P('occ', None, 'vir'), may hold values from -6 to 6
- integrals: bfloat16 [400, 400, 3200], P('vir', 'occ'), may hold values from -0.109375 to 0.109375
- batch_index: int32 [1], replicated, may hold values from 0 to 49
- eps_occ: float32 [40], replicated, may hold values from -1 to -0.3
- eps_vir: float32 [400], replicated, may hold values from 0.2 to 1.5
Outputs:
- update: float32 [400, 400, 1600], P(None, 'vir', 'occ')
Inputs may be any that keep to these rules, and one draw needn't show every extreme that they name: Selects the virtual orbitals d from 8 * batch_index to 8 * batch_index + 7.
All inputs are finite; a program needn't handle non-finite values.
Results may differ from a plain program's by a relative error of at most 0.0029.
Values may be sent and summed in bfloat16 or wider, within the bound.
A program may use at most 384 MiB of HBM per device.

v0:
```python
import jax
import jax.numpy as jnp
from jax import lax
from jax.sharding import PartitionSpec as P

NB = 8


def shards(amplitudes, integrals, batch_index, eps_occ, eps_vir):
    occ_rows = amplitudes.shape[0]
    occ_all = amplitudes.shape[1]
    vir_local = amplitudes.shape[2]
    block_a = integrals.shape[0]
    block_b = integrals.shape[1]
    begin = batch_index[0] * NB
    sliced = lax.dynamic_slice_in_dim(amplitudes, begin, NB, 3)
    sliced = sliced.reshape(occ_rows, occ_all, vir_local * NB)
    weights_flat = integrals.reshape(block_a * block_b, integrals.shape[2])
    dims_last = (((1,), (1,)), ((), ()))
    columns = lax.all_gather(sliced, "vir", axis=2, tiled=True)
    columns = columns.reshape(occ_rows * occ_all, columns.shape[2])
    ladder = lax.dot_general(
        weights_flat,
        lax.all_gather(columns, "occ", axis=0, tiled=True),
        dims_last,
        preferred_element_type=jnp.float32,
    )
    ladder = 0.5 * ladder.reshape(block_a, block_b, occ_all, occ_all)
    mixed = (ladder - jnp.transpose(ladder, (0, 1, 3, 2))).astype(jnp.bfloat16)
    mixed = mixed.reshape(block_a, block_b, occ_all * occ_all)
    relaid = lax.all_to_all(
        lax.all_to_all(mixed, "occ", split_axis=2, concat_axis=1, tiled=True),
        "vir",
        split_axis=1,
        concat_axis=0,
        tiled=True,
    )
    returned = lax.all_to_all(relaid, "vir", split_axis=0, concat_axis=1, tiled=True)
    mirrored = jnp.swapaxes(returned, 0, 1)
    pair_count = relaid.shape[2]
    pair_rows = pair_count // occ_all
    width_b = relaid.shape[1]
    occ_index = lax.axis_index("occ")
    vir_index = lax.axis_index("vir")
    energy_rows = lax.dynamic_slice_in_dim(eps_occ, occ_index * pair_rows, pair_rows, 0)
    pair_energy = (energy_rows[:, None] + eps_occ[None, :]).reshape(pair_count)
    energy_cols = lax.dynamic_slice_in_dim(eps_vir, vir_index * width_b, width_b, 0)
    denominator = pair_energy[None, None, :] - eps_vir[:, None, None] - energy_cols[None, :, None]
    return (relaid.astype(jnp.float32) - mirrored.astype(jnp.float32)) / denominator


def solution(mesh):
    in_specs = (P("occ", None, "vir", None), P("vir", "occ", None), P(), P(), P())
    out_specs = P(None, "vir", "occ")
    return jax.shard_map(shards, mesh=mesh, in_specs=in_specs, out_specs=out_specs, check_vma=False)
```

profile of v0, /device:TPU:0, one launch (start us, length us, event | category | flops | bytes accessed | tf_op | source)
XLA Modules:
  0.0 1750.7 jit_solution(14106090877960667524)
XLA Ops:
  7.2 6.2 constant_dynamic-slice_fusion
  13.4 4.9 copy.30
  18.4 56.2 %all-gather.3.cloned.1.call-done = bf16[10,40,3200]{1,2,0:T(8,128)(2,1)} async-done(((bf16[10,40,400]{1,2,0:T(8,128)(2,1)}), bf16[10,40,3200]{1,2,0:T(8,128)(2,1)}) %all-gather.3.cloned.1.call-update) | async-done | bytes 2560016 | tf_op jit(solution)/shard_map/all_gather | solution.py:20
  74.6 8.3 copy.31
  82.9 33.5 %reshape.69 = bf16[5000,3200]{1,0:T(8,128)(2,1)} reshape(bf16[50,100,3200]{2,1,0:T(8,128)(2,1)} %param.6) | data formatting | bytes 64000000 | tf_op jit(solution)/shard_map/reshape | solution.py:18
  116.4 146.5 %all-gather.5.cloned.1.call-done = bf16[1600,3200]{1,0:T(8,128)(2,1)} async-done(((bf16[400,3200]{1,0:T(8,128)(2,1)}), bf16[1600,3200]{1,0:T(8,128)(2,1)}) %all-gather.5.cloned.1.call-update) | async-done | bytes 10240016 | tf_op jit(solution)/shard_map/all_gather | solution.py:24
  263.0 65.0 %multiply_bitcast_fusion = f32[5000,1600]{0,1:T(8,128)} fusion(bf16[1600,3200]{1,0:T(8,128)(2,1)} %all-gather.5.cloned.1.call-done, bf16[5000,3200]{1,0:T(8,128)(2,1)} %reshape.69), kind=kOutput, calls=%fused_computation.4 | convolution fusion | flops 51207999488 | bytes 74240000 | tf_op jit(solution)/shard_map/dot_general | solution.py:22
  327.9 43.7 %mul.29 = f32[50,100,40,40]{1,0,3,2:T(8,128)} reshape(f32[5000,1600]{0,1:T(8,128)} %multiply_bitcast_fusion) | data formatting | bytes 64000000 | tf_op jit(solution)/shard_map/mul | solution.py:28
  371.7 36.6 %fusion = bf16[50,100,40,40]{1,0,3,2:T(8,128)(2,1)} fusion(f32[50,100,40,40]{1,0,3,2:T(8,128)} %mul.29), kind=kLoop, calls=%fused_computation.1 | loop fusion | flops 16000000 | bytes 48000000 | tf_op jit(solution)/shard_map/convert_element_type | solution.py:29
  408.3 509.0 %all_to_all.45 = bf16[50,100,1600]{1,0,2:T(8,128)(2,1)} all-to-all(bf16[50,100,1600]{1,0,2:T(8,128)(2,1)} %bitcast.31), channel_id=1, replica_groups=mesh['occ'=4,'vir'=8] {'occ'}, dimensions={2} | all-to-all | bytes 32000000 | tf_op jit(solution)/shard_map/all_to_all | solution.py:32
  917.3 35.0 %copy.41 = bf16[50,100,4,400]{3,2,1,0:T(4,128)(2,1)} copy(bf16[50,100,4,400]{1,0,3,2:T(8,128)(2,1)} %bitcast.32) | data formatting | bytes 32000000 | tf_op jit(solution)/shard_map/all_to_all | solution.py:32
  952.3 15.0 copy.42
  967.3 253.9 %all_to_all.46 = bf16[50,400,400]{2,0,1:T(8,128)(2,1)} all-to-all(bf16[50,400,400]{2,0,1:T(8,128)(2,1)S(1)} %bitcast.33), channel_id=1, replica_groups=mesh['occ'=4,'vir'=8] {'vir'}, dimensions={1} | all-to-all | bytes 32000000 | tf_op jit(solution)/shard_map/all_to_all | solution.py:31
  1221.2 16.3 copy.37
  1237.5 29.7 %all_to_all.40 = bf16[400,50,400]{2,0,1:T(8,128)(2,1)} reshape(bf16[8,50,50,400]{3,1,0,2:T(8,128)(2,1)} %copy.37) | data formatting | bytes 32000000 | tf_op jit(solution)/shard_map/all_to_all | solution.py:31
  1267.2 30.0 %copy.38 = bf16[400,50,400]{2,1,0:T(8,128)(2,1)} copy(bf16[400,50,400]{2,0,1:T(8,128)(2,1)} %all_to_all.40) | data formatting | bytes 32000000 | tf_op jit(solution)/shard_map/all_to_all | solution.py:31
  1297.2 6.6 all-to-all-start.2
  1304.1 0.1 broadcast_subtract_fusion
  1304.3 249.2 %all-to-all-done.2 = bf16[400,50,400]{2,1,0:T(8,128)(2,1)} async-done(((bf16[400,50,400]{2,1,0:T(8,128)(2,1)}), bf16[400,50,400]{2,1,0:T(8,128)(2,1)}, u32[]{:S(2)}, u32[]{:S(2)}) %all-to-all-start.2) | async-done | bytes 16000032 | tf_op jit(solution)/shard_map/all_to_all | solution.py:38
  1553.5 24.7 %copy_convert_fusion = f32[400,50,400]{2,0,1:T(8,128)} fusion(bf16[400,50,400]{2,1,0:T(8,128)(2,1)} %all-to-all-done.2), kind=kLoop, calls=%fused_computation.5 | loop fusion | flops 8000000 | bytes 48000000 | tf_op jit(solution)/shard_map/convert_element_type | solution.py:49
  1578.2 41.8 %reshape.72 = f32[8,50,50,400]{3,1,0,2:T(8,128)} reshape(f32[400,50,400]{2,0,1:T(8,128)} %copy_convert_fusion) | data formatting | bytes 64000000 | tf_op jit(solution)/shard_map/convert_element_type | solution.py:49
  1620.0 48.8 %copy.40 = f32[50,8,50,400]{3,2,1,0:T(8,128)} copy(f32[50,8,50,400]{3,0,1,2:T(8,128)} %bitcast.30) | data formatting | bytes 64000000 | tf_op jit(solution)/shard_map/convert_element_type | solution.py:49
  1668.8 41.8 %reshape.71 = f32[50,400,400]{2,1,0:T(8,128)} reshape(f32[50,8,50,400]{3,2,1,0:T(8,128)} %copy.40) | data formatting | bytes 64000000 | tf_op jit(solution)/shard_map/convert_element_type | solution.py:49
  1710.6 33.2 %fusion.1 = f32[400,50,400]{2,0,1:T(8,128)} fusion(f32[50,400,400]{2,1,0:T(8,128)} %reshape.71, bf16[400,50,400]{2,0,1:T(8,128)(2,1)} %all_to_all.40, f32[50]{0:T(128)S(1)} %dynamic_slice.11, f32[400,400]{1,0:T(8,128)S(1)} %broadcast_subtract_fusion), kind=kLoop, calls=%fused_computation.3 | loop fusion | flops 32000000 | bytes 80640200 | tf_op jit(solution)/shard_map/div | solution.py:49
  (12 shorter events, 0.4 us)
Async XLA Ops:
  6.5 68.1 %all-gather.3.cloned.1.call-start = ((), (), s32[]{:S(2)}) async-start(), calls=%async_computation.3 | async-start | bytes 9216000 | tf_op jit(solution)/shard_map/all_gather | solution.py:20
  18.3 244.6 %all-gather.5.cloned.1.call-start = ((), (), s32[]{:S(2)}) async-start(), calls=%async_computation.4 | async-start | bytes 12800000 | tf_op jit(solution)/shard_map/all_gather | solution.py:24
  1297.2 6.6 copy-start.1
  1297.2 6.9 copy-start
  1297.2 256.3 %all-to-all-start.2 = ((bf16[400,50,400]{2,1,0:T(8,128)(2,1)}), bf16[400,50,400]{2,1,0:T(8,128)(2,1)}, u32[]{:S(2)}, u32[]{:S(2)}) async-start(bf16[400,50,400]{2,1,0:T(8,128)(2,1)} %copy.38), calls=%async_computation.2 | async-start | bytes 45875200 | tf_op jit(solution)/shard_map/all_to_all | solution.py:38
Sparse Core Ops, SparseCore 0:
  18.5 56.1 all-gather.2
  83.1 179.8 all-gather.4
where the time goes:
time: 1760 us; the launch traced here: 1750 us
  blocking collectives  763 us (43%)
  waiting for transfers between devices  452 us (26%)
  local copies, waits for them, and re-layouts  355 us (20%)
  other arithmetic  94.7 us (5%)
  matrix products  65 us (4%)
    all_to_all x1, blocking collectives, shards(): lax.all_to_all(mixed, 'occ', split_axis=2, concat_axis=1, tiled=True)  509 us
    all_to_all x1, blocking collectives, shards(): lax.all_to_all(lax.all_to_all(mixed, 'occ', split_axis=2, concat_axis=1,...  254 us
    all_to_all x1, waiting for transfers between devices, shards(): lax.all_to_all(relaid, 'vir', split_axis=0, concat_axis=1, tiled=True)  249 us
    all_gather x1, waiting for transfers between devices, shards(): lax.all_gather(columns, 'occ', axis=0, tiled=True)  147 us
    convert_element_type x3, local copies, waits for them, and re-layouts, shards(): mirrored.astype(jnp.float32)  132 us
    all_to_all x3, local copies, waits for them, and re-layouts, shards(): lax.all_to_all(lax.all_to_all(mixed, 'occ', split_axis=2, concat_axis=1,...  76 us
    dot_general x1, matrix products, shards(): lax.dot_general(weights_flat, lax.all_gather(columns, 'occ', axis=0, tile...  65 us
    all_gather x1, waiting for transfers between devices, shards(): columns = lax.all_gather(sliced, 'vir', axis=2, tiled=True)  56.2 us
  transfers between devices with their start and end apart: 3, of which 3 were waited for; matrix products, arithmetic and copies ran while one was open for 2% of the time, Pallas kernels for 0%

commit v1 on v0

--- a/solution.py
+++ b/solution.py
@@ -4,6 +4,13 @@
 from jax.sharding import PartitionSpec as P
 
 NB = 8
+
+
+def advance_unit_here(s0):
+    high = lax.axis_size("vir")
+    tall = jnp.stack(jnp.split(s0, high, 1), axis=0)
+    wide_out = lax.all_to_all(tall, axis_name="vir", split_axis=0, concat_axis=0)
+    return jnp.concatenate(wide_out, 0)
 
 
 def shards(amplitudes, integrals, batch_index, eps_occ, eps_vir):
@@ -28,12 +35,8 @@
     ladder = 0.5 * ladder.reshape(block_a, block_b, occ_all, occ_all)
     mixed = (ladder - jnp.transpose(ladder, (0, 1, 3, 2))).astype(jnp.bfloat16)
     mixed = mixed.reshape(block_a, block_b, occ_all * occ_all)
-    relaid = lax.all_to_all(
-        lax.all_to_all(mixed, "occ", split_axis=2, concat_axis=1, tiled=True),
-        "vir",
-        split_axis=1,
-        concat_axis=0,
-        tiled=True,
+    relaid = advance_unit_here(
+        lax.all_to_all(mixed, "occ", split_axis=2, concat_axis=1, tiled=True)
     )
     returned = lax.all_to_all(relaid, "vir", split_axis=0, concat_axis=1, tiled=True)
     mirrored = jnp.swapaxes(returned, 0, 1)

time: 1760 us -> 1770 us (level)
    all_to_all x3 -> x1, local copies, waits for them, and re-layouts: 76 us -> 7.94 us  [advance_unit_here(): lax.all_to_all(tall, axis_name='vir', split_axis=0, concat_axis=0)]
    reshape x0 -> x2, local copies, waits for them, and re-layouts: none -> 59.7 us  [advance_unit_here(): return jnp.concatenate(wide_out, 0)]
    unnamed x4 -> x13, local copies, waits for them, and re-layouts: 0.01 us -> 21.4 us
    all_to_all x2 -> x1, local copies, waits for them, and re-layouts: 50 us -> 47.2 us  [shards(): lax.all_to_all(mixed, 'occ', split_axis=2, concat_axis=1, tiled=True)]
where the time goes in v1:
time: 1770 us; the launch traced here: 1760 us
  blocking collectives  763 us (43%)
  waiting for transfers between devices  452 us (26%)
  local copies, waits for them, and re-layouts  367 us (21%)
  other arithmetic  94.7 us (5%)
  matrix products  65 us (4%)
    all_to_all x1, blocking collectives, shards(): lax.all_to_all(mixed, 'occ', split_axis=2, concat_axis=1, tiled=True)  509 us
    all_to_all x1, blocking collectives, advance_unit_here(): lax.all_to_all(tall, axis_name='vir', split_axis=0, concat_axis=0)  254 us
    all_to_all x1, waiting for transfers between devices, shards(): lax.all_to_all(relaid, 'vir', split_axis=0, concat_axis=1, tiled=True)  249 us
    all_gather x1, waiting for transfers between devices, shards(): lax.all_gather(columns, 'occ', axis=0, tiled=True)  147 us
    convert_element_type x3, local copies, waits for them, and re-layouts, shards(): mirrored.astype(jnp.float32)  132 us
    dot_general x1, matrix products, shards(): lax.dot_general(weights_flat, lax.all_gather(columns, 'occ', axis=0, tile...  65 us
    reshape x2, local copies, waits for them, and re-layouts, advance_unit_here(): return jnp.concatenate(wide_out, 0)  59.7 us
    all_gather x1, waiting for transfers between devices, shards(): columns = lax.all_gather(sliced, 'vir', axis=2, tiled=True)  56.2 us
  transfers between devices with their start and end apart: 3, of which 3 were waited for; matrix products, arithmetic and copies ran while one was open for 2% of the time, Pallas kernels for 0%

profile of v1, /device:TPU:0, one launch (start us, length us, event | category | flops | bytes accessed | tf_op | source)
XLA Modules:
  0.0 1763.0 jit_solution(8494516812321461109)
XLA Ops:
  7.2 6.2 constant_dynamic-slice_fusion
  13.4 4.9 copy.47
  18.4 56.2 %all-gather.3.cloned.1.call-done = bf16[10,40,3200]{1,2,0:T(8,128)(2,1)} async-done(((bf16[10,40,400]{1,2,0:T(8,128)(2,1)}), bf16[10,40,3200]{1,2,0:T(8,128)(2,1)}) %all-gather.3.cloned.1.call-update) | async-done | bytes 2560016 | tf_op jit(solution)/shard_map/all_gather | solution.py:27
  74.6 8.3 copy.48
  82.9 33.5 %reshape.72 = bf16[5000,3200]{1,0:T(8,128)(2,1)} reshape(bf16[50,100,3200]{2,1,0:T(8,128)(2,1)} %param.6) | data formatting | bytes 64000000 | tf_op jit(solution)/shard_map/reshape | solution.py:25
  116.4 146.5 %all-gather.5.cloned.1.call-done = bf16[1600,3200]{1,0:T(8,128)(2,1)} async-done(((bf16[400,3200]{1,0:T(8,128)(2,1)}), bf16[1600,3200]{1,0:T(8,128)(2,1)}) %all-gather.5.cloned.1.call-update) | async-done | bytes 10240016 | tf_op jit(solution)/shard_map/all_gather | solution.py:31
  263.0 65.0 %multiply_bitcast_fusion = f32[5000,1600]{0,1:T(8,128)} fusion(bf16[1600,3200]{1,0:T(8,128)(2,1)} %all-gather.5.cloned.1.call-done, bf16[5000,3200]{1,0:T(8,128)(2,1)} %reshape.72), kind=kOutput, calls=%fused_computation.4 | convolution fusion | flops 51207999488 | bytes 74240000 | tf_op jit(solution)/shard_map/dot_general | solution.py:29
  327.9 43.7 %mul.29 = f32[50,100,40,40]{1,0,3,2:T(8,128)} reshape(f32[5000,1600]{0,1:T(8,128)} %multiply_bitcast_fusion) | data formatting | bytes 64000000 | tf_op jit(solution)/shard_map/mul | solution.py:35
  371.6 36.6 %fusion = bf16[50,100,40,40]{1,0,3,2:T(8,128)(2,1)} fusion(f32[50,100,40,40]{1,0,3,2:T(8,128)} %mul.29), kind=kLoop, calls=%fused_computation.1 | loop fusion | flops 16000000 | bytes 48000000 | tf_op jit(solution)/shard_map/convert_element_type | solution.py:36
  408.3 509.0 %all_to_all.32 = bf16[50,100,1600]{1,0,2:T(8,128)(2,1)} all-to-all(bf16[50,100,1600]{1,0,2:T(8,128)(2,1)} %bitcast.60), channel_id=1, replica_groups=mesh['occ'=4,'vir'=8] {'occ'}, dimensions={2} | all-to-all | bytes 32000000 | tf_op jit(solution)/shard_map/all_to_all | solution.py:39
  917.3 47.2 %copy.50 = bf16[50,100,4,400]{3,0,1,2:T(8,128)(2,1)} copy(bf16[50,100,4,400]{1,0,3,2:T(8,128)(2,1)} %bitcast.61) | data formatting | bytes 32000000 | tf_op jit(solution)/shard_map/all_to_all | solution.py:39
  968.2 4.4 fusion.8
  972.5 4.4 fusion.7
  987.6 254.2 %all_to_all.33 = bf16[8,50,50,400]{3,1,2,0:T(8,128)(2,1)S(1)} all-to-all(bf16[8,50,50,400]{3,1,2,0:T(8,128)(2,1)} %fusion.2), channel_id=1, replica_groups=mesh['occ'=4,'vir'=8] {'vir'}, dimensions={0} | all-to-all | bytes 32000000 | tf_op jit(solution)/shard_map/all_to_all | solution.py:12
  1241.9 7.9 copy.51
  1249.8 29.7 %reshape.74 = bf16[400,50,400]{2,0,1:T(8,128)(2,1)} reshape(bf16[8,50,50,400]{3,1,0,2:T(8,128)(2,1)} %copy.51) | data formatting | bytes 32000000 | tf_op jit(solution)/shard_map/reshape | solution.py:13
  1279.5 30.0 %copy.52 = bf16[400,50,400]{2,1,0:T(8,128)(2,1)} copy(bf16[400,50,400]{2,0,1:T(8,128)(2,1)} %reshape.74) | data formatting | bytes 32000000 | tf_op jit(solution)/shard_map/reshape | solution.py:13
  1309.5 6.6 all-to-all-start.2
  1316.6 249.2 %all-to-all-done.2 = bf16[400,50,400]{2,1,0:T(8,128)(2,1)} async-done(((bf16[400,50,400]{2,1,0:T(8,128)(2,1)}), bf16[400,50,400]{2,1,0:T(8,128)(2,1)}, u32[]{:S(2)}, u32[]{:S(2)}) %all-to-all-start.2) | async-done | bytes 16000032 | tf_op jit(solution)/shard_map/all_to_all | solution.py:41
  1565.8 24.7 %copy_convert_fusion = f32[400,50,400]{2,0,1:T(8,128)} fusion(bf16[400,50,400]{2,1,0:T(8,128)(2,1)} %all-to-all-done.2), kind=kLoop, calls=%fused_computation.5 | loop fusion | flops 8000000 | bytes 48000000 | tf_op jit(solution)/shard_map/convert_element_type | solution.py:52
  1590.5 41.8 %reshape.76 = f32[8,50,50,400]{3,1,0,2:T(8,128)} reshape(f32[400,50,400]{2,0,1:T(8,128)} %copy_convert_fusion) | data formatting | bytes 64000000 | tf_op jit(solution)/shard_map/convert_element_type | solution.py:52
  1632.3 48.8 %copy.54 = f32[50,8,50,400]{3,2,1,0:T(8,128)} copy(f32[50,8,50,400]{3,0,1,2:T(8,128)} %bitcast.59) | data formatting | bytes 64000000 | tf_op jit(solution)/shard_map/convert_element_type | solution.py:52
  1681.1 41.8 %reshape.75 = f32[50,400,400]{2,1,0:T(8,128)} reshape(f32[50,8,50,400]{3,2,1,0:T(8,128)} %copy.54) | data formatting | bytes 64000000 | tf_op jit(solution)/shard_map/convert_element_type | solution.py:52
  1722.9 33.2 %fusion.1 = f32[400,50,400]{2,0,1:T(8,128)} fusion(f32[50,400,400]{2,1,0:T(8,128)} %reshape.75, bf16[400,50,400]{2,0,1:T(8,128)(2,1)} %reshape.74, f32[50]{0:T(128)S(1)} %dynamic_slice.11, f32[400,400]{1,0:T(8,128)S(1)} %broadcast_subtract_fusion), kind=kLoop, calls=%fused_computation.3 | loop fusion | flops 32000000 | bytes 80640200 | tf_op jit(solution)/shard_map/div | solution.py:52
  (21 shorter events, 15.0 us)
Async XLA Ops:
  6.5 68.1 %all-gather.3.cloned.1.call-start = ((), (), s32[]{:S(2)}) async-start(), calls=%async_computation.3 | async-start | bytes 9216000 | tf_op jit(solution)/shard_map/all_gather | solution.py:27
  18.3 244.6 %all-gather.5.cloned.1.call-start = ((), (), s32[]{:S(2)}) async-start(), calls=%async_computation.4 | async-start | bytes 12800000 | tf_op jit(solution)/shard_map/all_gather | solution.py:31
  964.5 16.1 copy-start
  1309.5 6.6 copy-start.2
  1309.5 6.9 copy-start.1
  1309.5 256.3 %all-to-all-start.2 = ((bf16[400,50,400]{2,1,0:T(8,128)(2,1)}), bf16[400,50,400]{2,1,0:T(8,128)(2,1)}, u32[]{:S(2)}, u32[]{:S(2)}) async-start(bf16[400,50,400]{2,1,0:T(8,128)(2,1)} %copy.52), calls=%async_computation.2 | async-start | bytes 45875200 | tf_op jit(solution)/shard_map/all_to_all | solution.py:41
Sparse Core Ops, SparseCore 0:
  18.5 56.1 all-gather.2
  83.0 179.8 all-gather.4
